TPU v7x, 256 devices: a whole 4x4x8 slice. The times are simulated.
256 devices in a mesh: rep: 4 (over y), blk: 64 (over x, z, core).
Axes of the slice: x: 4, y: 4, z: 8, core: 2. Of those that a mesh axis runs over, the one named last changes fastest.
Arguments:
- feats: bfloat16 [1024, 128, 256], P('blk'), may hold values from -6 to 6
- requests: int32 [64, 64], P('blk'), may hold values from 0 to 15
- tile_dest: int32 [64, 512], P('blk'), may hold values from 0 to 15, as said below
- tile_slot: int32 [64, 512], P('blk'), may hold values from 0 to 63, as said below
- tile_vals: bfloat16 [64, 512, 128, 128], P('blk', None, 'rep'), may hold values from -0.09375 to 0.09375
- w_self: bfloat16 [256, 256], replicated, may hold values from -0.375 to 0.375
- w_neigh: bfloat16 [256, 256], replicated, may hold values from -0.375 to 0.375
- bias: float32 [256], replicated, may hold values from -3 to 3
- cotangent: bfloat16 [1024, 128, 256], P('blk', 'rep'), may hold values from -6 to 6
Outputs:
- hidden: bfloat16 [1024, 128, 256], P('blk', 'rep')
- grad_self: float32 [256, 256], replicated
- grad_neigh: float32 [256, 256], replicated
- grad_bias: float32 [256], replicated
- feat_grad: bfloat16 [1024, 128, 256], P('blk', 'rep')
Inputs may be any that keep to these rules, and one draw needn't show every extreme that they name: `tile_slot`: for each reader b, every owner index is named by exactly 8 of its tiles. `tile_dest`: no two tiles of one reader have both the same destination block and the same owner.
All inputs are finite; a program needn't handle non-finite values.
Results may differ from a plain program's by a relative error of at most 0.015.
Values may be sent and summed in bfloat16 or wider, within the bound.
A program may use at most 128 MiB of HBM per device.

v0:
```python
import math

import jax
import jax.numpy as jnp
from jax import lax
from jax.sharding import PartitionSpec as P


def collect_blocks(arrivals, send_list, blk_dev):
    onehot = (send_list[:, None] == jnp.arange(blk_dev, dtype=jnp.int32)[None, :]).astype(
        jnp.float32
    )
    return jnp.einsum("rb,rjd->bjd", onehot, arrivals, precision=lax.Precision.HIGHEST)


def on_device(feats, requests, tile_dest, tile_slot, tile_vals, w_self, w_neigh, bias, cotangent):
    owners = lax.axis_size("blk")
    replicas = lax.axis_size("rep")
    blk_dev, tile_rows, features = feats.shape
    quarter = tile_rows // replicas
    per_owner = blk_dev // 2
    rep_index = lax.axis_index("rep")
    send_list = requests[0]
    slot_owner = tile_slot[0]
    ordering = jnp.argsort(slot_owner, stable=True)
    sorted_dest = jnp.take(tile_dest[0], ordering, axis=0)
    grouped = jnp.take(tile_vals[0], ordering, axis=0).reshape(
        owners, per_owner, quarter, tile_rows
    )
    dest_onehot = sorted_dest[:, None] == jnp.arange(blk_dev, dtype=jnp.int32)[None, :]
    own_rows = lax.dynamic_slice_in_dim(feats, rep_index * quarter, quarter, 1)
    outgoing = jnp.take(feats, send_list, axis=0)
    sources = lax.all_to_all(outgoing, "blk", split_axis=0, concat_axis=0, tiled=True)
    products = jnp.einsum("okij,ojd->okid", grouped, sources, preferred_element_type=jnp.float32)
    products = products.reshape(owners * per_owner, quarter * features)
    summed = jnp.dot(dest_onehot.astype(jnp.float32).T, products, precision=lax.Precision.HIGHEST)
    aggregate = summed.reshape(blk_dev, quarter, features).astype(jnp.bfloat16)
    row_count = blk_dev * quarter
    feat_rows = own_rows.reshape(row_count, features)
    agg_rows = aggregate.reshape(row_count, features)
    preact = jnp.dot(feat_rows, w_self, preferred_element_type=jnp.float32)
    preact = preact + jnp.dot(agg_rows, w_neigh, preferred_element_type=jnp.float32) + bias
    hidden = jax.nn.silu(preact).astype(jnp.bfloat16).reshape(blk_dev, quarter, features)
    gating = jax.nn.sigmoid(preact)
    grad_rows = cotangent.reshape(row_count, features).astype(jnp.float32)
    grad_pre = (grad_rows * gating * (1.0 + preact * (1.0 - gating))).astype(jnp.bfloat16)
    grad_scale = 1.0 / math.sqrt(owners * blk_dev * tile_rows)
    self_local = (
        jnp.einsum("nd,ne->de", feat_rows, grad_pre, preferred_element_type=jnp.float32)
        * grad_scale
    )
    neigh_local = (
        jnp.einsum("nd,ne->de", agg_rows, grad_pre, preferred_element_type=jnp.float32) * grad_scale
    )
    bias_local = jnp.sum(grad_pre.astype(jnp.float32), axis=0) * grad_scale
    grad_self, grad_neigh, grad_bias = lax.psum(
        (self_local, neigh_local, bias_local), ("rep", "blk")
    )
    back_rows = jnp.einsum(
        "ne,de->nd", grad_pre, w_neigh, preferred_element_type=jnp.float32
    ).astype(jnp.bfloat16)
    back_flat = back_rows.reshape(blk_dev, quarter * features)
    picked = jnp.dot(
        dest_onehot.astype(jnp.bfloat16), back_flat, preferred_element_type=jnp.float32
    ).astype(jnp.bfloat16)
    picked = picked.reshape(owners, per_owner, quarter, features)
    contributions = jnp.einsum(
        "okij,okid->ojd", grouped, picked, preferred_element_type=jnp.float32
    )
    self_term = jnp.einsum("ne,de->nd", grad_pre, w_self, preferred_element_type=jnp.float32)
    arrivals = lax.all_to_all(
        contributions.astype(jnp.bfloat16), "blk", split_axis=0, concat_axis=0, tiled=True
    ).astype(contributions.dtype)
    collected = collect_blocks(arrivals, send_list, blk_dev)
    neighbour = lax.psum_scatter(
        collected.astype(jnp.bfloat16), "rep", scatter_dimension=1, tiled=True
    ).astype(jnp.float32)
    feat_grad = (self_term.reshape(blk_dev, quarter, features) + neighbour).astype(jnp.bfloat16)
    return (hidden, grad_self, grad_neigh, grad_bias, feat_grad)


def solution(mesh):
    in_specs = (
        P("blk", None, None),
        P("blk", None),
        P("blk", None),
        P("blk", None),
        P("blk", None, "rep", None),
        P(),
        P(),
        P(),
        P("blk", "rep", None),
    )
    out_specs = (P("blk", "rep", None), P(), P(), P(), P("blk", "rep", None))
    return jax.shard_map(
        on_device, mesh=mesh, in_specs=in_specs, out_specs=out_specs, check_vma=False
    )
```

profile of v0, /device:TPU:1, one launch (start us, length us, event | category | flops | bytes accessed | tf_op | source)
XLA Modules:
  0.0 564.1 jit_solution(1460504856205556514)
XLA Ops:
  8.0 0.0 copy-start
  8.0 0.7 fusion.23
  8.8 0.7 compare_and_fusion
  9.4 0.0 copy-done
  9.4 2.8 gather_fusion.2
  12.2 4.6 broadcast_select_fusion
  16.8 0.0 copy-start.6
  16.8 0.0 copy-start.2
  16.8 13.3 %all-to-all-start = ((bf16[64,128,256]{2,1,0:T(8,128)(2,1)}), bf16[64,128,256]{2,1,0:T(8,128)(2,1)}, u32[]{:S(2)}, u32[]{:S(2)}) async-start(bf16[64,128,256]{2,1,0:T(8,128)(2,1)} %broadcast_select_fusion), calls=%async_computation | async-start | bytes 8388608 | tf_op jit(solution)/shard_map/all_to_all | solution.py:33
  30.1 0.0 reduce-scatter.2.cloned.1.call-start
  30.2 0.0 copy-done.6
  30.2 3.8 sort.17
  34.0 0.0 copy-done.2
  34.0 3.5 gather_fusion
  37.5 0.1 broadcast_in_dim.36
  37.6 0.0 copy-start.4
  37.6 5.5 gather_fusion.1
  43.1 0.0 copy-done.4
  43.2 0.2 fusion.27
  43.4 82.6 %all-to-all-done = bf16[64,128,256]{2,1,0:T(8,128)(2,1)} async-done(((bf16[64,128,256]{2,1,0:T(8,128)(2,1)}), bf16[64,128,256]{2,1,0:T(8,128)(2,1)}, u32[]{:S(2)}, u32[]{:S(2)}) %all-to-all-start) | async-done | bytes 4194336 | tf_op jit(solution)/shard_map/all_to_all | solution.py:33
  126.0 4.9 convolution_bitcast_fusion
  130.9 17.9 %copy.29 = f32[64,8,32,256]{3,1,2,0:T(8,128)} copy(f32[64,8,32,256]{3,2,1,0:T(8,128)S(1)} %convolution_bitcast_fusion) | data formatting | bytes 33554432
  148.8 17.5 %copy.21 = f32[8192,512]{1,0:T(8,128)} copy(f32[8192,512]{0,1:T(8,128)} %bitcast.56) | data formatting | bytes 33554432 | tf_op jit(solution)/shard_map/dot_general | solution.py:36
  166.3 0.0 copy-start.5
  166.3 0.0 copy-start.8
  166.3 0.0 copy-start.9
  166.3 11.3 %convolution_convert_fusion.1 = bf16[16,32,256]{2,0,1:T(8,128)(2,1)S(1)} fusion(f32[32,256,512]{2,1,0:T(8,128)} %bitcast.55, s32[512]{0:T(512)S(1)} %get-tuple-element.26), kind=kOutput, calls=%fused_computation.18 | convolution fusion | flops 805445632 | bytes 17041408 | tf_op jit(solution)/shard_map/dot_general | solution.py:36
  177.6 0.1 copy.22
  177.7 0.0 copy-done.5
  177.7 0.0 copy-done.8
  177.7 0.0 copy-done.9
  177.7 1.1 convert_reduce_fusion
  178.9 0.3 convolution_convert_fusion.2
  179.1 0.1 reshape.89
  179.3 0.0 copy-start.3
  179.3 5.6 convolution_convert_fusion
  184.9 0.0 copy-done.3
  184.9 8.3 %bitcast_convert_fusion = bf16[64,128,256]{2,1,0:T(8,128)(2,1)} fusion(bf16[64,8,32,256]{3,1,2,0:T(8,128)(2,1)} %bitcast.59, bf16[64,8,32,128]{3,2,1,0:T(8,128)(2,1)S(1)} %bitcast.58, pred[64,8]{1,0:T(8,128)(4,1)S(1)} %broadcast_in_dim.36), kind=kOutput, calls=%fused_computation.5 | convolution fusion | flops 1077936128 | bytes 16777728 | tf_op jit(solution)/shard_map/okij,okid->ojd/dot_general | solution.py:67
  193.2 0.0 copy-start.7
  193.2 102.1 %all_to_all.10 = bf16[64,128,256]{2,1,0:T(8,128)(2,1)S(1)} all-to-all(bf16[64,128,256]{2,1,0:T(8,128)(2,1)} %bitcast_convert_fusion), channel_id=1, replica_groups=mesh['rep'=4,'blk'=64] {'blk'}, dimensions={0} | all-to-all | bytes 8388608 | tf_op jit(solution)/shard_map/all_to_all | solution.py:71
  295.3 0.0 copy-done.7
  295.3 0.0 copy-start.1
  295.3 3.3 fusion.9
  298.6 0.0 reduce-scatter.2.cloned.1.call-update
  298.6 0.0 all-reduce.3.cloned.1.call-start
  298.7 1.0 convolution_multiply_fusion
  299.6 1.0 convolution_multiply_fusion.1
  300.6 0.3 fusion.28
  300.9 0.0 all-reduce.3.cloned.1.call-update
  300.9 77.1 %psum.23 = f32[256]{0:T(256)} all-reduce(f32[256]{0:T(256)S(1)} %broadcast_multiply_fusion), channel_id=1, replica_groups=mesh['rep'=4,'blk'=64] {'rep','blk'}, use_global_device_ids=true, to_apply=%region_4.5 | all-reduce | flops 256 | bytes 2048 | tf_op jit(solution)/shard_map/psum | solution.py:56
  378.0 0.0 reduce-scatter.2.cloned.1.call-done
  378.0 1.2 fusion.15
  379.3 0.8 copy.26
  380.0 173.2 %all-reduce.3.cloned.1.call-done = (f32[256,256]{1,0:T(8,128)}, f32[256,256]{1,0:T(8,128)}) async-done(((f32[256,256]{1,0:T(8,128)}, f32[256,256]{1,0:T(8,128)}), (f32[256,256]{1,0:T(8,128)}, f32[256,256]{1,0:T(8,128)})) %all-reduce.3.cloned.1.call-update) | async-done | bytes 524304 | tf_op jit(solution)/shard_map/psum | solution.py:56
  553.3 1.7 copy.43
  554.9 1.7 copy.44
  556.6 0.0 copy-done.1
  (7 shorter events, 0.0 us)
Async XLA Ops:
  8.0 1.4 copy-start
  16.8 13.4 %copy-start.6 = (s32[1,512]{1,0:T(1,128)S(1)}, s32[1,512]{1,0:T(1,128)}, u32[]{:S(2)}) copy-start(s32[1,512]{1,0:T(1,128)} %param.12) | copy-start | bytes 6148
  16.8 17.2 %copy-start.2 = (s32[1,512]{1,0:T(1,128)S(1)}, s32[1,512]{1,0:T(1,128)}, u32[]{:S(2)}) copy-start(s32[1,512]{1,0:T(1,128)} %param.11) | copy-start | bytes 6148
  16.8 109.2 %all-to-all-start = ((bf16[64,128,256]{2,1,0:T(8,128)(2,1)}), bf16[64,128,256]{2,1,0:T(8,128)(2,1)}, u32[]{:S(2)}, u32[]{:S(2)}) async-start(bf16[64,128,256]{2,1,0:T(8,128)(2,1)} %broadcast_select_fusion), calls=%async_computation | async-start | bytes 8388608 | tf_op jit(solution)/shard_map/all_to_all | solution.py:33
  30.1 347.9 %reduce-scatter.2.cloned.1.call-start = ((), (), s32[]{:S(2)}) async-start(), calls=%async_computation.3 | async-start | bytes 1310720 | tf_op jit(solution)/shard_map/reduce_scatter | solution.py:75
  37.6 5.5 copy-start.4
  166.3 11.4 %copy-start.5 = (bf16[256,256]{1,0:T(8,128)(2,1)S(1)}, bf16[256,256]{1,0:T(8,128)(2,1)}, u32[]{:S(2)}) copy-start(bf16[256,256]{1,0:T(8,128)(2,1)} %param.15) | copy-start | bytes 393220
  166.3 11.4 %copy-start.8 = (bf16[16,32,256]{2,1,0:T(8,128)(2,1)S(1)}, bf16[16,32,256]{2,1,0:T(8,128)(2,1)}, u32[]{:S(2)}) copy-start(bf16[16,32,256]{2,1,0:T(8,128)(2,1)} %param.17) | copy-start | bytes 786436
  166.3 11.4 %copy-start.9 = (f32[256]{0:T(256)S(1)}, f32[256]{0:T(256)}, u32[]{:S(2)}) copy-start(f32[256]{0:T(256)} %param.16) | copy-start | bytes 3076
  179.3 5.6 copy-start.3
  193.2 102.1 %copy-start.7 = (s32[1,64]{1,0:T(1,128)S(1)}, s32[1,64]{1,0:T(1,128)}, u32[]{:S(2)}) copy-start(s32[1,64]{1,0:T(1,128)} %param.10) | copy-start | bytes 772
  295.3 261.4 %copy-start.1 = (bf16[16,128,256]{2,1,0:T(8,128)(2,1)S(1)}, bf16[16,128,256]{2,1,0:T(8,128)(2,1)}, u32[]{:S(2)}) copy-start(bf16[16,128,256]{2,1,0:T(8,128)(2,1)} %param.9) | copy-start | bytes 3145732
  298.6 254.7 %all-reduce.3.cloned.1.call-start = ((), (), s32[]{:S(2)}) async-start(), calls=%async_computation.4 | async-start | bytes 1048576 | tf_op jit(solution)/shard_map/psum | solution.py:56
Sparse Core Ops, SparseCore 0:
  298.7 21.3 reduce-scatter.1
Sparse Core Ops, SparseCore 1:
  305.3 247.9 all-reduce.2
where the time goes:
time: 565 us; the launch traced here: 564 us
  waiting for transfers between devices  256 us (45%)
  blocking collectives  179 us (32%)
  local copies, waits for them, and re-layouts  51.6 us (9%)
  matrix products  37.3 us (7%)
  between operations  15.7 us (3%)
  starting transfers between devices  13.4 us (2%)
  other arithmetic  11.1 us (2%)
    psum x1, waiting for transfers between devices, on_device(): lax.psum((self_local, neigh_local, bias_local), ('rep', 'blk'))  173 us
    all_to_all x1, blocking collectives, on_device(): lax.all_to_all(contributions.astype(jnp.bfloat16), 'blk', split_axis=0, c...  102 us
    all_to_all x1, waiting for transfers between devices, on_device(): lax.all_to_all(outgoing, 'blk', split_axis=0, concat_axis=0, tiled=True)  82.6 us
    psum x1, blocking collectives, on_device(): lax.psum((self_local, neigh_local, bias_local), ('rep', 'blk'))  77.1 us
    unnamed x24, local copies, waits for them, and re-layouts  22.1 us
    dot_general x1, local copies, waits for them, and re-layouts, on_device(): jnp.dot(dest_onehot.astype(jnp.float32).T, products, precision=lax.Precis...  17.5 us
    all_to_all x1, starting transfers between devices, on_device(): lax.all_to_all(outgoing, 'blk', split_axis=0, concat_axis=0, tiled=True)  13.3 us
    dot_general x1, matrix products, on_device(): jnp.dot(dest_onehot.astype(jnp.float32).T, products, precision=lax.Precis...  11.3 us
  transfers between devices with their start and end apart: 3, of which 2 were waited for; matrix products, arithmetic and copies ran while one was open for 3% of the time, Pallas kernels for 0%

commit v1 on v0

v1 whole, which is shorter than its diff:
```python
import functools
import math

import jax
import jax.numpy as jnp
from jax import lax
from jax.experimental import pallas as pl
from jax.experimental.pallas import tpu as pltpu
from jax.sharding import PartitionSpec as P

SPLIT = (4, 8, 2)
CHUNK = 4
LAG = 3

MESH = pl.DeviceIdType.MESH
F32 = jnp.float32
BF16 = jnp.bfloat16


def exchange_kernel(
    split,
    chunk,
    scale,
    req_ref,
    inv_ref,
    feats_ref,
    tiles_ref,
    ws_ref,
    wn_ref,
    bias_ref,
    ct_ref,
    hid_out,
    fg_out,
    grad_out,
    own,
    ct,
    tv,
    stage,
    src,
    tden,
    acc,
    gp,
    agg,
    back,
    hid,
    fg,
    cf,
    r1s,
    r1r,
    r2s,
    r2r,
    r3s,
    arr,
    g_all,
    g_core,
    g_xs,
    g_zs,
    g_piece,
    g_ys,
    g_fz,
    g_fx,
    g_fc,
    in_sem,
    out_sem,
    a_send,
    a_recv,
    b1_send,
    b1_recv,
    b2_send,
    b2_recv,
    r1_send,
    r1_recv,
    r2_send,
    r2_recv,
    r3_send,
    r3_recv,
    gc_send,
    gc_recv,
    gx_send,
    gx_recv,
    gz_send,
    gz_recv,
    gy_send,
    gy_recv,
    hz_send,
    hz_recv,
    hx_send,
    hx_recv,
    hc_send,
    hc_recv,
):
    nx, nz, nc = split
    slots = nx * nz * nc
    steps = slots // chunk
    y = lax.axis_index("rep")
    b = lax.axis_index("blk")
    x = lax.div(b, nz * nc)
    z = lax.rem(lax.div(b, nc), nz)
    c = lax.rem(b, nc)
    up = lax.rem(y + 1, 4)
    down = lax.rem(y + 3, 4)
    far = lax.rem(y + 2, 4)

    def shift(s):
        dc = lax.rem(s, nc)
        p = lax.div(s, nc)
        dx = lax.rem(p, nx)
        q = lax.div(p, nx)
        dz = lax.div(q + 1, 2) * (2 * lax.rem(q, 2) - 1)
        return dx, dz, dc

    def at(px, pz, pc):
        return (px * nz + pz) * nc + pc

    def reader(s):
        dx, dz, dc = shift(s)
        return at(lax.rem(x + dx, nx), lax.rem(z + dz + nz, nz), lax.rem(c + dc, nc))

    def owner(s):
        dx, dz, dc = shift(s)
        return at(
            lax.rem(x - dx + nx, nx), lax.rem(z - dz + nz, nz), lax.rem(c - dc + nc, nc)
        )

    def remote(source, target, send, recv, rep, blk):
        return pltpu.make_async_remote_copy(
            src_ref=source,
            dst_ref=target,
            send_sem=send,
            recv_sem=recv,
            device_id=(rep, blk),
            device_id_type=MESH,
        )

    load_own = pltpu.make_async_copy(feats_ref.at[:, y], own, in_sem.at[0])
    load_tiles = pltpu.make_async_copy(
        tiles_ref, tv.at[pl.ds(0, tiles_ref.shape[0])], in_sem.at[1]
    )
    load_ct = pltpu.make_async_copy(ct_ref, ct, in_sem.at[2])
    load_own.start()
    load_tiles.start()
    load_ct.start()

    barrier = pltpu.get_barrier_semaphore()

    def greet(s, carry):
        pl.semaphore_signal(barrier, inc=1, device_id=(y, reader(s)), device_id_type=MESH)
        return carry

    lax.fori_loop(1, slots, greet, 0)
    for d in range(1, 4):
        pl.semaphore_signal(
            barrier, inc=1, device_id=(lax.rem(y + d, 4), b), device_id_type=MESH
        )
    tv[tiles_ref.shape[0]] = jnp.zeros(tv.shape[1:], BF16)
    load_own.wait()

    def gather(s, carry):
        stage[s] = own[req_ref[reader(s)]]
        return carry

    lax.fori_loop(0, slots, gather, 0)
    src[0, y] = stage[0]
    acc[...] = jnp.zeros_like(acc)
    pl.semaphore_wait(barrier, slots - 1 + 3)

    def a_copy(s):
        return remote(
            stage.at[s], src.at[s, y], a_send.at[s], a_recv.at[s], y, reader(s)
        )

    def a_start(s, carry):
        a_copy(s).start()
        return carry

    lax.fori_loop(1, slots, a_start, 0)
    load_tiles.wait()

    def b1_copy(i, d):
        part = src.at[pl.ds(i * chunk, chunk), y]
        return remote(
            part, part, b1_send.at[i, d], b1_recv.at[i, d], (up, down)[d], b
        )

    def b1_wait(i, d):
        part = src.at[pl.ds(i * chunk, chunk), (down, up)[d]]
        remote(part, part, b1_send.at[i, d], b1_recv.at[i, d], (up, down)[d], b).wait_recv()

    def b2_copy(i, d):
        part = src.at[pl.ds(i * chunk, chunk), (down, up)[d], d]
        return remote(
            part, part, b2_send.at[i, d], b2_recv.at[i, d], (up, down)[d], b
        )

    def b2_wait(i, d):
        part = src.at[pl.ds(i * chunk, chunk), far, d]
        remote(part, part, b2_send.at[i, d], b2_recv.at[i, d], (up, down)[d], b).wait_recv()

    blocks = own.shape[0]
    rows = own.shape[1] * own.shape[2]
    width = 4 * rows
    feat = own.shape[-1]
    total = blocks * rows

    def forward(i, carry):
        @pl.when(i < steps)
        def _():
            @pl.when(i >= 0)
            def _():
                for k in range(chunk):
                    s = i * chunk + k
                    o = owner(s)
                    for d in range(blocks):
                        tden[i, pl.ds(d * rows, rows), pl.ds(k * width, width)] = tv[
                            inv_ref[d * slots + o]
                        ]

            for k in range(chunk):
                s = i * chunk + k

                @pl.when(s > 0)
                def _():
                    a_copy(s).wait_recv()

            for d in range(2):
                b1_copy(i, d).start()

        @pl.when(jnp.logical_and(i >= 1, i < steps + 1))
        def _():
            for d in range(2):
                b1_wait(i - 1, d)
            for d in range(2):
                b2_copy(i - 1, d).start()

        @pl.when(i >= 2)
        def _():
            for d in range(2):
                b2_wait(i - 2, d)
            blockset = src[pl.ds((i - 2) * chunk, chunk)].reshape(chunk * width, feat)
            acc[...] += jnp.dot(tden[i - 2], blockset, preferred_element_type=F32)

        return carry

    lax.fori_loop(0, steps + 2, forward, 0)

    load_ct.wait()
    part = total // 4
    per = blocks // 4

    def dense(n, carry):
        here = pl.ds(n * part, part)
        blk = pl.ds(n * per, per)
        mine = own[blk].reshape(part, feat)
        mixed = acc[here, :].astype(BF16)
        agg[here, :] = mixed
        pre = jnp.dot(mine, ws_ref[...], preferred_element_type=F32)
        pre = pre + jnp.dot(mixed, wn_ref[...], preferred_element_type=F32) + bias_ref[...]
        gate = 1.0 / (1.0 + jnp.exp(-pre))
        hid[blk] = (pre * gate).astype(BF16).reshape(per, rows, feat)
        down_grad = ct[blk].reshape(part, feat).astype(F32)
        grad = (down_grad * gate * (1.0 + pre * (1.0 - gate))).astype(BF16)
        gp[here, :] = grad
        back[here, :] = lax.dot_general(
            grad, wn_ref[...], (((1,), (1,)), ((), ())), preferred_element_type=F32
        ).astype(BF16)
        return carry

    lax.fori_loop(0, 4, dense, 0)
    save_hid = pltpu.make_async_copy(hid, hid_out, out_sem.at[0])
    save_hid.start()

    def r1_copy(j, d):
        here = pl.ds(j * chunk, chunk)
        return remote(
            r1s.at[here, d],
            r1r.at[here, d],
            r1_send.at[j, d],
            r1_recv.at[j, d],
            (up, down)[d],
            b,
        )

    def r2_copy(j, d):
        here = pl.ds(j * chunk, chunk)
        return remote(
            r2s.at[here, d],
            r2r.at[here, d],
            r2_send.at[j, d],
            r2_recv.at[j, d],
            (up, down)[d],
            b,
        )

    def r3_copy(s):
        return remote(r3s.at[s], arr.at[s], r3_send.at[s], r3_recv.at[s], y, owner(s))

    half = nx * nz
    other = at(x, z, nc - 1 - c) if nc == 2 else b

    def core_copy():
        return remote(
            g_all.at[pl.ds((1 - c) * half, half)], g_core, gc_send, gc_recv, y, other
        )

    def x_copy(d):
        peer = lax.rem(x + d, nx)
        return remote(
            g_all.at[pl.ds(c * half + peer * nz, nz)],
            g_xs.at[d],
            gx_send.at[d],
            gx_recv.at[d],
            y,
            at(peer, z, c),
        )

    def z_copy(d):
        peer = lax.rem(z + d, nz)
        return remote(
            g_all.at[c * half + x * nz + peer],
            g_zs.at[d],
            gz_send.at[d],
            gz_recv.at[d],
            y,
            at(x, peer, c),
        )

    def y_copy(d):
        return remote(
            g_piece, g_ys.at[y], gy_send.at[d], gy_recv.at[d], lax.rem(y + d, 4), b
        )

    def zz_copy(d):
        return remote(
            g_fz.at[z],
            g_fz.at[z],
            hz_send.at[d],
            hz_recv.at[d],
            y,
            at(x, lax.rem(z + d, nz), c),
        )

    def xx_copy(d):
        return remote(
            g_fz, g_fx.at[x], hx_send.at[d], hx_recv.at[d], y, at(lax.rem(x + d, nx), z, c)
        )

    def cc_copy():
        return remote(g_fx, g_fc.at[c], hc_send, hc_recv, y, other)

    def grads():
        feat_rows = own[...].reshape(total, feat)
        grad = gp[...]
        first = lax.dot_general(
            feat_rows, grad, (((0,), (0,)), ((), ())), preferred_element_type=F32
        )
        second = lax.dot_general(
            agg[...], grad, (((0,), (0,)), ((), ())), preferred_element_type=F32
        )
        pieces = nc * half
        tall = 2 * feat // pieces
        g_all[...] = jnp.zeros_like(g_all)
        g_all[pl.ds(0, pieces // 2), pl.ds(0, tall), :] = (first * scale).reshape(
            pieces // 2, tall, feat
        )
        g_all[pl.ds(pieces // 2, pieces // 2), pl.ds(0, tall), :] = (second * scale).reshape(
            pieces // 2, tall, feat
        )
        g_all[0, pl.ds(tall, 1), :] = (
            jnp.sum(grad.astype(F32), axis=0, keepdims=True) * scale
        )
        if nc == 2:
            core_copy().start()

    def grads_core():
        if nc == 2:
            core_copy().wait_recv()
            here = pl.ds(c * half, half)
            g_all[here] = g_all[here] + g_core[...]
        for d in range(1, nx):
            x_copy(d).start()

    def grads_x():
        here = pl.ds(c * half + x * nz, nz)
        value = g_all[here]
        for d in range(1, nx):
            x_copy(d).wait_recv()
            value = value + g_xs[d]
        g_all[here] = value
        for d in range(1, nz):
            z_copy(d).start()

    def grads_z():
        value = g_all[c * half + x * nz + z]
        for d in range(1, nz):
            z_copy(d).wait_recv()
            value = value + g_zs[d]
        g_piece[...] = value
        g_ys[y] = value
        for d in range(1, 4):
            y_copy(d).start()

    def grads_y():
        for d in range(1, 4):
            source = lax.rem(y + 4 - d, 4)
            remote(
                g_piece, g_ys.at[source], gy_send.at[d], gy_recv.at[d], y, b
            ).wait_recv()
        g_fz[z] = (g_ys[0] + g_ys[1]) + (g_ys[2] + g_ys[3])
        for d in range(1, nz):
            zz_copy(d).start()

    def grads_zz():
        for d in range(1, nz):
            source = lax.rem(z + nz - d, nz)
            remote(
                g_fz.at[z], g_fz.at[source], hz_send.at[d], hz_recv.at[d], y, b
            ).wait_recv()
        g_fx[x] = g_fz[...]
        for d in range(1, nx):
            xx_copy(d).start()

    def grads_xx():
        for d in range(1, nx):
            source = lax.rem(x + nx - d, nx)
            remote(
                g_fz, g_fx.at[source], hx_send.at[d], hx_recv.at[d], y, b
            ).wait_recv()
        g_fc[c] = g_fx[...]
        if nc == 2:
            cc_copy().start()

    def grads_cc():
        if nc == 2:
            remote(g_fx, g_fc.at[1 - c], hc_send, hc_recv, y, b).wait_recv()

    def collect(j):
        lane = lax.broadcasted_iota(jnp.int32, (1, chunk * rows), 1)
        target = lax.rem(lane, rows)
        for k in range(chunk):
            s = j * chunk + k
            inside = jnp.logical_and(lane >= k * rows, lane < (k + 1) * rows)
            target = target + jnp.where(inside, req_ref[reader(s)] * rows, 0)

            @pl.when(s > 0)
            def _():
                r3_copy(s).wait_recv()

        row = lax.broadcasted_iota(jnp.int32, (total, chunk * rows), 0)
        pick = jnp.where(row == target, 1.0, 0.0).astype(BF16)
        came = arr[pl.ds(j * chunk, chunk)].reshape(chunk * rows, feat)
        acc[...] += jnp.dot(pick, came, preferred_element_type=F32)

    stages = (grads_core, grads_x, grads_z, grads_y, grads_zz, grads_xx)

    def backward(i, carry):
        j = steps - 1 - i

        @pl.when(i < steps)
        def _():
            product = lax.dot_general(
                tden[j], back[...], (((0,), (0,)), ((), ())), preferred_element_type=F32
            )
            here = pl.ds(j * chunk, chunk)
            cf[...] = product.reshape(chunk, 4, 2, rows // 2, feat)
            r1s[here] = cf[:, far].astype(BF16)
            r2s[here, 0] = cf[:, up].astype(BF16)
            r2s[here, 1] = cf[:, down].astype(BF16)
            r3s[here] = cf[:, y].astype(BF16)
            for d in range(2):
                r1_copy(j, d).start()

        @pl.when(jnp.logical_and(i >= 1, i < steps + 1))
        def _():
            n = j + 1
            here = pl.ds(n * chunk, chunk)
            for d in range(2):
                r1_copy(n, d).wait_recv()
                r2s[here, d, d] = (
                    r2s[here, d, d].astype(F32) + r1r[here, d].astype(F32)
                ).astype(BF16)
            for d in range(2):
                r2_copy(n, d).start()

        @pl.when(jnp.logical_and(i >= 2, i < steps + 2))
        def _():
            n = j + 2
            here = pl.ds(n * chunk, chunk)
            for d in range(2):
                r2_copy(n, d).wait_recv()
            r3s[here] = (
                r3s[here].astype(F32) + r2r[here, 0].astype(F32) + r2r[here, 1].astype(F32)
            ).astype(BF16)
            for k in range(chunk):
                s = n * chunk + k

                @pl.when(s > 0)
                def _():
                    r3_copy(s).start()

        @pl.when(i == 0)
        def _():
            grads()
            grad = gp[...]
            acc[...] = lax.dot_general(
                grad, ws_ref[...], (((1,), (1,)), ((), ())), preferred_element_type=F32
            )

        for n, stage_fn in enumerate(stages):

            @pl.when(i == min(2 + 2 * n, steps + 1))
            def _(stage_fn=stage_fn):
                stage_fn()

        @pl.when(i >= 2 + LAG)
        def _():
            collect(j + 2 + LAG)

        return carry

    lax.fori_loop(0, steps + 2, backward, 0)
    arr[0] = r3s[0]
    for n in range(LAG):
        if LAG - 1 - n < steps:
            collect(jnp.int32(LAG - 1 - n))
    fg[...] = acc[...].astype(BF16).reshape(fg.shape)
    save_fg = pltpu.make_async_copy(fg, fg_out, out_sem.at[1])
    save_fg.start()
    grads_cc()
    save_grad = pltpu.make_async_copy(g_fc, grad_out, out_sem.at[2])
    save_grad.start()

    def sent(s, carry):
        a_copy(s).wait_send()
        r3_copy(s).wait_send()
        return carry

    lax.fori_loop(1, slots, sent, 0)

    def sent_y(i, carry):
        for d in range(2):
            b1_copy(i, d).wait_send()
            b2_copy(i, d).wait_send()
            r1_copy(i, d).wait_send()
            r2_copy(i, d).wait_send()
        return carry

    lax.fori_loop(0, steps, sent_y, 0)
    if nc == 2:
        core_copy().wait_send()
        cc_copy().wait_send()
    for d in range(1, nx):
        x_copy(d).wait_send()
        xx_copy(d).wait_send()
    for d in range(1, nz):
        z_copy(d).wait_send()
        zz_copy(d).wait_send()
    for d in range(1, 4):
        y_copy(d).wait_send()
    save_hid.wait()
    save_fg.wait()
    save_grad.wait()


def finish_kernel(pieces, tall, grad_ref, hid_ref, fg_ref, hid_o, gs_o, gn_o, gb_o, fg_o):
    feat = grad_ref.shape[-1]
    value = grad_ref[...]
    gs_o[...] = value[: pieces // 2, :tall, :].reshape(feat, feat)
    gn_o[...] = value[pieces // 2 :, :tall, :].reshape(feat, feat)
    gb_o[...] = value[0, tall : tall + 1, :]
    hid_o[...] = hid_ref[...]
    fg_o[...] = fg_ref[...]


def on_device(feats, requests, tile_dest, tile_slot, tile_vals, w_self, w_neigh, bias, cotangent):
    owners = lax.axis_size("blk")
    replicas = lax.axis_size("rep")
    nx, nz, nc = SPLIT
    chunk = CHUNK
    steps = owners // chunk
    blocks, tile_rows, feat = feats.shape
    rows = tile_rows // replicas
    total = blocks * rows
    tiles = tile_vals.shape[1]
    pieces = nc * nx * nz
    tall = 2 * feat // pieces
    scale = 1.0 / math.sqrt(owners * blocks * tile_rows)

    number = jnp.arange(tiles, dtype=jnp.int32)
    hit = jnp.logical_and(
        tile_dest[0][None, None, :] == jnp.arange(blocks, dtype=jnp.int32)[:, None, None],
        tile_slot[0][None, None, :] == jnp.arange(owners, dtype=jnp.int32)[None, :, None],
    )
    inverse = tiles + jnp.sum(jnp.where(hit, number - tiles, 0), axis=-1)
    inverse = inverse.reshape(blocks * owners)

    vmem = pltpu.VMEM
    sem = pltpu.SemaphoreType.DMA
    piece = (tall + 1, feat)
    scratch = [
        vmem((blocks, 2, rows // 2, feat), BF16),
        vmem((blocks, rows, feat), BF16),
        vmem((tiles + 1, rows, tile_rows), BF16),
        vmem((owners, 2, rows // 2, feat), BF16),
        vmem((owners, 4, 2, rows // 2, feat), BF16),
        vmem((steps, total, chunk * tile_rows), BF16),
        vmem((total, feat), F32),
        vmem((total, feat), BF16),
        vmem((total, feat), BF16),
        vmem((total, feat), BF16),
        vmem((blocks, rows, feat), BF16),
        vmem((blocks, rows, feat), BF16),
        vmem((chunk, 4, 2, rows // 2, feat), F32),
        vmem((owners, 2, rows // 2, feat), BF16),
        vmem((owners, 2, rows // 2, feat), BF16),
        vmem((owners, 2, 2, rows // 2, feat), BF16),
        vmem((owners, 2, 2, rows // 2, feat), BF16),
        vmem((owners, 2, rows // 2, feat), BF16),
        vmem((owners, 2, rows // 2, feat), BF16),
        vmem((pieces, *piece), F32),
        vmem((nx * nz, *piece), F32),
        vmem((nx, nz, *piece), F32),
        vmem((nz, *piece), F32),
        vmem(piece, F32),
        vmem((4, *piece), F32),
        vmem((nz, *piece), F32),
        vmem((nx, nz, *piece), F32),
        vmem((nc, nx, nz, *piece), F32),
        sem((3,)),
        sem((3,)),
        sem((owners,)),
        sem((owners,)),
        sem((steps, 2)),
        sem((steps, 2)),
        sem((steps, 2)),
        sem((steps, 2)),
        sem((steps, 2)),
        sem((steps, 2)),
        sem((steps, 2)),
        sem((steps, 2)),
        sem((owners,)),
        sem((owners,)),
        sem,
        sem,
        sem((nx,)),
        sem((nx,)),
        sem((nz,)),
        sem((nz,)),
        sem((4,)),
        sem((4,)),
        sem((nz,)),
        sem((nz,)),
        sem((nx,)),
        sem((nx,)),
        sem,
        sem,
    ]
    smem = pl.BlockSpec(memory_space=pltpu.SMEM)
    hbm = pl.BlockSpec(memory_space=pl.ANY)
    whole = pl.BlockSpec(memory_space=pltpu.VMEM)
    hid, fg, grad = pl.pallas_call(
        functools.partial(exchange_kernel, SPLIT, chunk, scale),
        out_shape=(
            jax.ShapeDtypeStruct((blocks, rows, feat), BF16),
            jax.ShapeDtypeStruct((blocks, rows, feat), BF16),
            jax.ShapeDtypeStruct((nc, nx, nz, *piece), F32),
        ),
        in_specs=[smem, smem, hbm, hbm, whole, whole, whole, hbm],
        out_specs=(hbm, hbm, hbm),
        scratch_shapes=scratch,
        compiler_params=pltpu.CompilerParams(
            collective_id=0, has_side_effects=True, vmem_limit_bytes=60 << 20
        ),
    )(
        requests[0],
        inverse,
        feats.reshape(blocks, replicas, 2, rows // 2, feat),
        tile_vals[0],
        w_self,
        w_neigh,
        bias.reshape(1, feat),
        cotangent,
    )
    hidden, grad_self, grad_neigh, grad_bias, feat_grad = pl.pallas_call(
        functools.partial(finish_kernel, pieces, tall),
        out_shape=(
            jax.ShapeDtypeStruct((blocks, rows, feat), BF16),
            jax.ShapeDtypeStruct((feat, feat), F32),
            jax.ShapeDtypeStruct((feat, feat), F32),
            jax.ShapeDtypeStruct((1, feat), F32),
            jax.ShapeDtypeStruct((blocks, rows, feat), BF16),
        ),
        in_specs=[whole, whole, whole],
        out_specs=(whole, whole, whole, whole, whole),
    )(grad.reshape(pieces, *piece), hid, fg)
    return (hidden, grad_self, grad_neigh, grad_bias.reshape(feat), feat_grad)


def solution(mesh):
    in_specs = (
        P("blk", None, None),
        P("blk", None),
        P("blk", None),
        P("blk", None),
        P("blk", None, "rep", None),
        P(),
        P(),
        P(),
        P("blk", "rep", None),
    )
    out_specs = (P("blk", "rep", None), P(), P(), P(), P("blk", "rep", None))
    return jax.shard_map(
        on_device, mesh=mesh, in_specs=in_specs, out_specs=out_specs, check_vma=False
    )
```

time: 565 us -> 142 us (0.25)
  waiting for transfers between devices: 256 us -> 0 us
  blocking collectives: 179 us -> 0 us
  Pallas kernels: 0 us -> 139 us
  local copies, waits for them, and re-layouts: 51.6 us -> 0.67 us
  matrix products: 37.3 us -> 0 us
  between operations: 15.7 us -> 0.65 us
  starting transfers between devices: 13.4 us -> 0 us
  other arithmetic: 11.1 us -> 1.81 us
    psum x1 -> x0, waiting for transfers between devices: 173 us -> none  [on_device(): lax.psum((self_local, neigh_local, bias_local), ('rep', 'blk'))]
    pallas_call x0 -> x2, Pallas kernels: none -> 139 us  [the longest x1 136 us: on_device(): pl.pallas_call(functools.partial(exchange_kernel, SPLIT, chunk, scale), o...]
    all_to_all x1 -> x0, blocking collectives: 102 us -> none  [on_device(): lax.all_to_all(contributions.astype(jnp.bfloat16), 'blk', split_axis=0, c...]
    all_to_all x1 -> x0, waiting for transfers between devices: 82.6 us -> none  [on_device(): lax.all_to_all(outgoing, 'blk', split_axis=0, concat_axis=0, tiled=True)]
    psum x1 -> x0, blocking collectives: 77.1 us -> none  [on_device(): lax.psum((self_local, neigh_local, bias_local), ('rep', 'blk'))]
    dot_general x11 -> x0, matrix products: 37.3 us -> none  [the longest x1 11.3 us: on_device(): jnp.dot(dest_onehot.astype(jnp.float32).T, products, precision=lax.Precis...]
    unnamed x24 -> x0, local copies, waits for them, and re-layouts: 22.1 us -> none
    dot_general x1 -> x0, local copies, waits for them, and re-layouts: 17.5 us -> none  [on_device(): jnp.dot(dest_onehot.astype(jnp.float32).T, products, precision=lax.Precis...]
  transfers between devices with their start and end apart: 3 -> 0, of which waited for: 2 -> 0; matrix products, arithmetic and copies ran while one was open for 3% -> 0% of each run, Pallas kernels for 0% -> 0%
where the time goes in v1:
time: 142 us
  Pallas kernels  139 us (98%)
  other arithmetic  1.81 us (1%)
    pallas_call x1, Pallas kernels, on_device(): pl.pallas_call(functools.partial(exchange_kernel, SPLIT, chunk, scale), o...  136 us

profile of v1, /device:TPU:1, one launch (start us, length us, event | category | flops | bytes accessed | tf_op | source)
XLA Modules:
  0.0 141.8 jit_solution(18361691825886560)
XLA Ops:
  0.6 0.7 iota_compare_fusion.1
  1.3 0.7 iota_compare_fusion
  2.0 0.4 select_reduce_fusion
  2.5 0.7 add.13.inv_ref
  3.1 136.3 %shard_map.131 = (bf16[16,32,256]{2,1,0:T(8,128)(2,1)}, bf16[16,32,256]{2,1,0:T(8,128)(2,1)}, f32[2,4,8,9,256]{4,3,2,1,0:T(8,128)}) custom-call(s32[64]{0:T(128)} %bitcast.14, s32[1024]{0:T(1024)} %add.13.inv_ref, bf16[16,4,2,16,256]{4,3,2,1,0:T(8,128)(2,1)} %bitcast.10, bf16[512,32,128]{2,1,0:T(8,128)(2,1)} %bitcast.8, bf16[256,256]{1,0:T(8,128)(2,1)} %ws_ref.1, ...), custom_call_target="tpu_custom_call" | custom-call | tf_op jit(solution)/shard_map/pallas_call | solution.py:660
  139.5 2.3 %shard_map.132 = (bf16[16,32,256]{2,1,0:T(8,128)(2,1)}, f32[256,256]{1,0:T(8,128)}, f32[256,256]{1,0:T(8,128)}, f32[1,256]{1,0:T(1,128)}, bf16[16,32,256]{2,1,0:T(8,128)(2,1)}) custom-call(f32[64,9,256]{2,1,0:T(8,128)} %bitcast.9, bf16[16,32,256]{2,1,0:T(8,128)(2,1)} %get-tuple-element.14.hid_ref, bf16[16,32,256]{2,1,0:T(8,128)(2,1)} %get-tuple-element.15.fg_ref), custom_call_target="tpu_custom_call" | custom-call | tf_op jit(solution)/shard_map/pallas_call | solution.py:683
  (2 shorter events, 0.0 us)

commit v2 on v1

--- a/solution.py
+++ b/solution.py
@@ -10,7 +10,10 @@
 
 SPLIT = (4, 8, 2)
 CHUNK = 4
-LAG = 3
+LAG = 5
+HOP1, HOP2 = 2, 4
+
+GRADS_AT, GRADS_GAP = 3, 2
 
 MESH = pl.DeviceIdType.MESH
 F32 = jnp.float32
@@ -32,10 +35,11 @@
     hid_out,
     fg_out,
     grad_out,
-    own,
+    fv,
     ct,
     tv,
     stage,
+    stage_near,
     src,
     tden,
     acc,
@@ -64,6 +68,8 @@
     out_sem,
     a_send,
     a_recv,
+    near_send,
+    near_recv,
     b1_send,
     b1_recv,
     b2_send,
@@ -92,6 +98,8 @@
     nx, nz, nc = split
     slots = nx * nz * nc
     steps = slots // chunk
+    near = nx * nc
+    skip = near // chunk
     y = lax.axis_index("rep")
     b = lax.axis_index("blk")
     x = lax.div(b, nz * nc)
@@ -132,7 +140,7 @@
             device_id_type=MESH,
         )
 
-    load_own = pltpu.make_async_copy(feats_ref.at[:, y], own, in_sem.at[0])
+    load_own = pltpu.make_async_copy(feats_ref, fv, in_sem.at[0])
     load_tiles = pltpu.make_async_copy(
         tiles_ref, tv.at[pl.ds(0, tiles_ref.shape[0])], in_sem.at[1]
     )
@@ -156,92 +164,99 @@
     load_own.wait()
 
     def gather(s, carry):
-        stage[s] = own[req_ref[reader(s)]]
-        return carry
-
-    lax.fori_loop(0, slots, gather, 0)
-    src[0, y] = stage[0]
+        stage[s] = fv[req_ref[reader(s)], y]
+        return carry
+
+    lax.fori_loop(near, slots, gather, 0)
+
+    def gather_near(s, carry):
+        stage_near[s] = fv[req_ref[reader(s)]]
+        return carry
+
+    lax.fori_loop(1, near, gather_near, 0)
+    src[0] = fv[req_ref[b]]
     acc[...] = jnp.zeros_like(acc)
+    blocks = fv.shape[0]
+    rows = fv.shape[2] * fv.shape[3]
+    width = 4 * rows
+    feat = fv.shape[-1]
+    total = blocks * rows
+    load_tiles.wait()
+
+    def spread(i, carry):
+        for k in range(chunk):
+            o = owner(i * chunk + k)
+            for d in range(blocks):
+                tden[i, pl.ds(d * rows, rows), pl.ds(k * width, width)] = tv[
+                    inv_ref[d * slots + o]
+                ]
+        return carry
+
+    lax.fori_loop(0, steps, spread, 0)
     pl.semaphore_wait(barrier, slots - 1 + 3)
 
     def a_copy(s):
         return remote(
-            stage.at[s], src.at[s, y], a_send.at[s], a_recv.at[s], y, reader(s)
+            stage.at[s], src.at[s, y], a_send, a_recv.at[lax.div(s, chunk)], y, reader(s)
         )
 
     def a_start(s, carry):
         a_copy(s).start()
         return carry
 
-    lax.fori_loop(1, slots, a_start, 0)
-    load_tiles.wait()
+    lax.fori_loop(near, slots, a_start, 0)
+
+    def near_start(s, carry):
+        remote(stage_near.at[s], src.at[s], near_send, near_recv, y, reader(s)).start()
+        return carry
+
+    lax.fori_loop(1, near, near_start, 0)
+
+    def wait_recv(target, recv):
+        remote(target, target, in_sem.at[0], recv, up, b).wait_recv()
+
+    def wait_send(source, send):
+        remote(source, source, send, in_sem.at[0], up, b).wait_send()
 
     def b1_copy(i, d):
         part = src.at[pl.ds(i * chunk, chunk), y]
-        return remote(
-            part, part, b1_send.at[i, d], b1_recv.at[i, d], (up, down)[d], b
-        )
-
-    def b1_wait(i, d):
-        part = src.at[pl.ds(i * chunk, chunk), (down, up)[d]]
-        remote(part, part, b1_send.at[i, d], b1_recv.at[i, d], (up, down)[d], b).wait_recv()
+        return remote(part, part, b1_send, b1_recv.at[i], (up, down)[d], b)
 
     def b2_copy(i, d):
         part = src.at[pl.ds(i * chunk, chunk), (down, up)[d], d]
-        return remote(
-            part, part, b2_send.at[i, d], b2_recv.at[i, d], (up, down)[d], b
-        )
-
-    def b2_wait(i, d):
-        part = src.at[pl.ds(i * chunk, chunk), far, d]
-        remote(part, part, b2_send.at[i, d], b2_recv.at[i, d], (up, down)[d], b).wait_recv()
-
-    blocks = own.shape[0]
-    rows = own.shape[1] * own.shape[2]
-    width = 4 * rows
-    feat = own.shape[-1]
-    total = blocks * rows
+        return remote(part, part, b2_send, b2_recv.at[i], (up, down)[d], b)
+
+    def mix(i):
+        blockset = src[pl.ds(i * chunk, chunk)].reshape(chunk * width, feat)
+        acc[...] += jnp.dot(tden[i], blockset, preferred_element_type=F32)
 
     def forward(i, carry):
         @pl.when(i < steps)
         def _():
-            @pl.when(i >= 0)
-            def _():
-                for k in range(chunk):
-                    s = i * chunk + k
-                    o = owner(s)
-                    for d in range(blocks):
-                        tden[i, pl.ds(d * rows, rows), pl.ds(k * width, width)] = tv[
-                            inv_ref[d * slots + o]
-                        ]
-
-            for k in range(chunk):
-                s = i * chunk + k
-
-                @pl.when(s > 0)
-                def _():
-                    a_copy(s).wait_recv()
-
+            wait_recv(src.at[pl.ds(i * chunk, chunk), y], a_recv.at[i])
             for d in range(2):
                 b1_copy(i, d).start()
 
-        @pl.when(jnp.logical_and(i >= 1, i < steps + 1))
-        def _():
+        @pl.when(jnp.logical_and(i >= skip + HOP1, i < steps + HOP1))
+        def _():
+            wait_recv(src.at[pl.ds((i - HOP1) * chunk, chunk), pl.ds(0, 2)], b1_recv.at[i - HOP1])
             for d in range(2):
-                b1_wait(i - 1, d)
-            for d in range(2):
-                b2_copy(i - 1, d).start()
-
-        @pl.when(i >= 2)
-        def _():
-            for d in range(2):
-                b2_wait(i - 2, d)
-            blockset = src[pl.ds((i - 2) * chunk, chunk)].reshape(chunk * width, feat)
-            acc[...] += jnp.dot(tden[i - 2], blockset, preferred_element_type=F32)
-
-        return carry
-
-    lax.fori_loop(0, steps + 2, forward, 0)
+                b2_copy(i - HOP1, d).start()
+
+        @pl.when(i >= skip + HOP2)
+        def _():
+            wait_recv(src.at[pl.ds((i - HOP2) * chunk, chunk), far], b2_recv.at[i - HOP2])
+            mix(i - HOP2)
+
+        @pl.when(i == steps // 2)
+        def _():
+            wait_recv(src.at[pl.ds(1, near - 1)], near_recv)
+            for n in range(skip):
+                mix(n)
+
+        return carry
+
+    lax.fori_loop(skip, steps + HOP2, forward, 0)
 
     load_ct.wait()
     part = total // 4
@@ -250,7 +265,7 @@
     def dense(n, carry):
         here = pl.ds(n * part, part)
         blk = pl.ds(n * per, per)
-        mine = own[blk].reshape(part, feat)
+        mine = fv[blk, y].reshape(part, feat)
         mixed = acc[here, :].astype(BF16)
         agg[here, :] = mixed
         pre = jnp.dot(mine, ws_ref[...], preferred_element_type=F32)
@@ -274,8 +289,8 @@
         return remote(
             r1s.at[here, d],
             r1r.at[here, d],
-            r1_send.at[j, d],
-            r1_recv.at[j, d],
+            r1_send,
+            r1_recv.at[j],
             (up, down)[d],
             b,
         )
@@ -285,14 +300,16 @@
         return remote(
             r2s.at[here, d],
             r2r.at[here, d],
-            r2_send.at[j, d],
-            r2_recv.at[j, d],
+            r2_send,
+            r2_recv.at[j],
             (up, down)[d],
             b,
         )
 
     def r3_copy(s):
-        return remote(r3s.at[s], arr.at[s], r3_send.at[s], r3_recv.at[s], y, owner(s))
+        return remote(
+            r3s.at[s], arr.at[s], r3_send, r3_recv.at[lax.div(s, chunk)], y, owner(s)
+        )
 
     half = nx * nz
     other = at(x, z, nc - 1 - c) if nc == 2 else b
@@ -307,8 +324,8 @@
         return remote(
             g_all.at[pl.ds(c * half + peer * nz, nz)],
             g_xs.at[d],
-            gx_send.at[d],
-            gx_recv.at[d],
+            gx_send,
+            gx_recv,
             y,
             at(peer, z, c),
         )
@@ -318,22 +335,22 @@
         return remote(
             g_all.at[c * half + x * nz + peer],
             g_zs.at[d],
-            gz_send.at[d],
-            gz_recv.at[d],
+            gz_send,
+            gz_recv,
             y,
             at(x, peer, c),
         )
 
     def y_copy(d):
         return remote(
-            g_piece, g_ys.at[y], gy_send.at[d], gy_recv.at[d], lax.rem(y + d, 4), b
+            g_piece, g_ys.at[y], gy_send, gy_recv.at[d], lax.rem(y + d, 4), b
         )
 
     def zz_copy(d):
         return remote(
             g_fz.at[z],
             g_fz.at[z],
-            hz_send.at[d],
+            hz_send,
             hz_recv.at[d],
             y,
             at(x, lax.rem(z + d, nz), c),
@@ -341,14 +358,14 @@
 
     def xx_copy(d):
         return remote(
-            g_fz, g_fx.at[x], hx_send.at[d], hx_recv.at[d], y, at(lax.rem(x + d, nx), z, c)
+            g_fz, g_fx.at[x], hx_send, hx_recv.at[d], y, at(lax.rem(x + d, nx), z, c)
         )
 
     def cc_copy():
         return remote(g_fx, g_fc.at[c], hc_send, hc_recv, y, other)
 
     def grads():
-        feat_rows = own[...].reshape(total, feat)
+        feat_rows = fv[:, y].reshape(total, feat)
         grad = gp[...]
         first = lax.dot_general(
             feat_rows, grad, (((0,), (0,)), ((), ())), preferred_element_type=F32
@@ -358,16 +375,16 @@
         )
         pieces = nc * half
         tall = 2 * feat // pieces
-        g_all[...] = jnp.zeros_like(g_all)
-        g_all[pl.ds(0, pieces // 2), pl.ds(0, tall), :] = (first * scale).reshape(
+        g_all[:, :, pl.ds(feat, 128)] = jnp.zeros((pieces, tall, 128), F32)
+        g_all[pl.ds(0, pieces // 2), :, pl.ds(0, feat)] = (first * scale).reshape(
             pieces // 2, tall, feat
         )
-        g_all[pl.ds(pieces // 2, pieces // 2), pl.ds(0, tall), :] = (second * scale).reshape(
+        g_all[pl.ds(pieces // 2, pieces // 2), :, pl.ds(0, feat)] = (second * scale).reshape(
             pieces // 2, tall, feat
         )
-        g_all[0, pl.ds(tall, 1), :] = (
-            jnp.sum(grad.astype(F32), axis=0, keepdims=True) * scale
-        )
+        down_sum = jnp.sum(grad.astype(F32), axis=0, keepdims=True) * scale
+        for n in range(feat // 128):
+            g_all[0, pl.ds(n, 1), pl.ds(feat, 128)] = down_sum[:, n * 128 : (n + 1) * 128]
         if nc == 2:
             core_copy().start()
 
@@ -382,8 +399,8 @@
     def grads_x():
         here = pl.ds(c * half + x * nz, nz)
         value = g_all[here]
+        wait_recv(g_xs.at[pl.ds(1, nx - 1)], gx_recv)
         for d in range(1, nx):
-            x_copy(d).wait_recv()
             value = value + g_xs[d]
         g_all[here] = value
         for d in range(1, nz):
@@ -391,8 +408,8 @@
 
     def grads_z():
         value = g_all[c * half + x * nz + z]
+        wait_recv(g_zs.at[pl.ds(1, nz - 1)], gz_recv)
         for d in range(1, nz):
-            z_copy(d).wait_recv()
             value = value + g_zs[d]
         g_piece[...] = value
         g_ys[y] = value
@@ -402,9 +419,7 @@
     def grads_y():
         for d in range(1, 4):
             source = lax.rem(y + 4 - d, 4)
-            remote(
-                g_piece, g_ys.at[source], gy_send.at[d], gy_recv.at[d], y, b
-            ).wait_recv()
+            wait_recv(g_ys.at[source], gy_recv.at[d])
         g_fz[z] = (g_ys[0] + g_ys[1]) + (g_ys[2] + g_ys[3])
         for d in range(1, nz):
             zz_copy(d).start()
@@ -412,9 +427,7 @@
     def grads_zz():
         for d in range(1, nz):
             source = lax.rem(z + nz - d, nz)
-            remote(
-                g_fz.at[z], g_fz.at[source], hz_send.at[d], hz_recv.at[d], y, b
-            ).wait_recv()
+            wait_recv(g_fz.at[source], hz_recv.at[d])
         g_fx[x] = g_fz[...]
         for d in range(1, nx):
             xx_copy(d).start()
@@ -422,16 +435,14 @@
     def grads_xx():
         for d in range(1, nx):
             source = lax.rem(x + nx - d, nx)
-            remote(
-                g_fz, g_fx.at[source], hx_send.at[d], hx_recv.at[d], y, b
-            ).wait_recv()
+            wait_recv(g_fx.at[source], hx_recv.at[d])
         g_fc[c] = g_fx[...]
         if nc == 2:
             cc_copy().start()
 
     def grads_cc():
         if nc == 2:
-            remote(g_fx, g_fc.at[1 - c], hc_send, hc_recv, y, b).wait_recv()
+            wait_recv(g_fc.at[1 - c], hc_recv)
 
     def collect(j):
         lane = lax.broadcasted_iota(jnp.int32, (1, chunk * rows), 1)
@@ -441,9 +452,13 @@
             inside = jnp.logical_and(lane >= k * rows, lane < (k + 1) * rows)
             target = target + jnp.where(inside, req_ref[reader(s)] * rows, 0)
 
-            @pl.when(s > 0)
-            def _():
-                r3_copy(s).wait_recv()
+        @pl.when(j > 0)
+        def _():
+            wait_recv(arr.at[pl.ds(j * chunk, chunk)], r3_recv.at[j])
+
+        @pl.when(j == 0)
+        def _():
+            wait_recv(arr.at[pl.ds(1, chunk - 1)], r3_recv.at[0])
 
         row = lax.broadcasted_iota(jnp.int32, (total, chunk * rows), 0)
         pick = jnp.where(row == target, 1.0, 0.0).astype(BF16)
@@ -452,11 +467,18 @@
 
     stages = (grads_core, grads_x, grads_z, grads_y, grads_zz, grads_xx)
 
+    def turn(i):
+        n = lax.div(i, skip)
+        odd = lax.rem(n, 2)
+        early = nz - 1 - lax.div(n, 2)
+        late = lax.rem(lax.div(n + 1, 2), nz // 2)
+        return ((1 - odd) * early + odd * late) * skip + lax.rem(i, skip)
+
     def backward(i, carry):
-        j = steps - 1 - i
 
         @pl.when(i < steps)
         def _():
+            j = turn(i)
             product = lax.dot_general(
                 tden[j], back[...], (((0,), (0,)), ((), ())), preferred_element_type=F32
             )
@@ -469,24 +491,23 @@
             for d in range(2):
                 r1_copy(j, d).start()
 
-        @pl.when(jnp.logical_and(i >= 1, i < steps + 1))
-        def _():
-            n = j + 1
+        @pl.when(jnp.logical_and(i >= HOP1, i < steps + HOP1))
+        def _():
+            n = turn(i - HOP1)
             here = pl.ds(n * chunk, chunk)
+            wait_recv(r1r.at[here], r1_recv.at[n])
             for d in range(2):
-                r1_copy(n, d).wait_recv()
                 r2s[here, d, d] = (
                     r2s[here, d, d].astype(F32) + r1r[here, d].astype(F32)
                 ).astype(BF16)
             for d in range(2):
                 r2_copy(n, d).start()
 
-        @pl.when(jnp.logical_and(i >= 2, i < steps + 2))
-        def _():
-            n = j + 2
+        @pl.when(jnp.logical_and(i >= HOP2, i < steps + HOP2))
+        def _():
+            n = turn(i - HOP2)
             here = pl.ds(n * chunk, chunk)
-            for d in range(2):
-                r2_copy(n, d).wait_recv()
+            wait_recv(r2r.at[here], r2_recv.at[n])
             r3s[here] = (
                 r3s[here].astype(F32) + r2r[here, 0].astype(F32) + r2r[here, 1].astype(F32)
             ).astype(BF16)
@@ -497,9 +518,16 @@
                 def _():
                     r3_copy(s).start()
 
-        @pl.when(i == 0)
+                @pl.when(s == 0)
+                def _():
+                    arr[0] = r3s[0]
+
+        @pl.when(i == GRADS_AT)
         def _():
             grads()
+
+        @pl.when(i == GRADS_AT - 1)
+        def _():
             grad = gp[...]
             acc[...] = lax.dot_general(
                 grad, ws_ref[...], (((1,), (1,)), ((), ())), preferred_element_type=F32
@@ -507,21 +535,19 @@
 
         for n, stage_fn in enumerate(stages):
 
-            @pl.when(i == min(2 + 2 * n, steps + 1))
+            @pl.when(i == min(GRADS_AT + GRADS_GAP * (n + 1), steps + HOP2 - 1))
             def _(stage_fn=stage_fn):
                 stage_fn()
 
-        @pl.when(i >= 2 + LAG)
-        def _():
-            collect(j + 2 + LAG)
-
-        return carry
-
-    lax.fori_loop(0, steps + 2, backward, 0)
-    arr[0] = r3s[0]
+        @pl.when(i >= HOP2 + LAG)
+        def _():
+            collect(turn(i - HOP2 - LAG))
+
+        return carry
+
+    lax.fori_loop(0, steps + HOP2, backward, 0)
     for n in range(LAG):
-        if LAG - 1 - n < steps:
-            collect(jnp.int32(LAG - 1 - n))
+        collect(turn(jnp.int32(steps - LAG + n)))
     fg[...] = acc[...].astype(BF16).reshape(fg.shape)
     save_fg = pltpu.make_async_copy(fg, fg_out, out_sem.at[1])
     save_fg.start()
@@ -529,44 +555,33 @@
     save_grad = pltpu.make_async_copy(g_fc, grad_out, out_sem.at[2])
     save_grad.start()
 
-    def sent(s, carry):
-        a_copy(s).wait_send()
-        r3_copy(s).wait_send()
-        return carry
-
-    lax.fori_loop(1, slots, sent, 0)
-
-    def sent_y(i, carry):
-        for d in range(2):
-            b1_copy(i, d).wait_send()
-            b2_copy(i, d).wait_send()
-            r1_copy(i, d).wait_send()
-            r2_copy(i, d).wait_send()
-        return carry
-
-    lax.fori_loop(0, steps, sent_y, 0)
+    wait_send(stage.at[pl.ds(near, slots - near)], a_send)
+    wait_send(stage_near.at[pl.ds(1, near - 1)], near_send)
+    wait_send(src.at[pl.ds(near, slots - near), pl.ds(0, 2)], b1_send)
+    wait_send(src.at[pl.ds(near, slots - near), 0], b2_send)
+    wait_send(r1s, r1_send)
+    wait_send(r2s, r2_send)
+    wait_send(r3s.at[pl.ds(1, slots - 1)], r3_send)
     if nc == 2:
         core_copy().wait_send()
         cc_copy().wait_send()
-    for d in range(1, nx):
-        x_copy(d).wait_send()
-        xx_copy(d).wait_send()
-    for d in range(1, nz):
-        z_copy(d).wait_send()
-        zz_copy(d).wait_send()
-    for d in range(1, 4):
-        y_copy(d).wait_send()
+    wait_send(g_xs.at[pl.ds(1, nx - 1)], gx_send)
+    wait_send(g_zs.at[pl.ds(1, nz - 1)], gz_send)
+    wait_send(g_ys.at[pl.ds(0, 3)], gy_send)
+    wait_send(g_fz.at[pl.ds(0, nz - 1)], hz_send)
+    wait_send(g_fx.at[pl.ds(0, nx - 1)], hx_send)
     save_hid.wait()
     save_fg.wait()
     save_grad.wait()
 
 
-def finish_kernel(pieces, tall, grad_ref, hid_ref, fg_ref, hid_o, gs_o, gn_o, gb_o, fg_o):
-    feat = grad_ref.shape[-1]
-    value = grad_ref[...]
-    gs_o[...] = value[: pieces // 2, :tall, :].reshape(feat, feat)
-    gn_o[...] = value[pieces // 2 :, :tall, :].reshape(feat, feat)
-    gb_o[...] = value[0, tall : tall + 1, :]
+def finish_kernel(grad_ref, hid_ref, fg_ref, hid_o, gs_o, gn_o, gb_o, fg_o):
+    pieces = grad_ref.shape[0]
+    feat = gs_o.shape[0]
+    gs_o[...] = grad_ref[pl.ds(0, pieces // 2), :, pl.ds(0, feat)].reshape(feat, feat)
+    gn_o[...] = grad_ref[pl.ds(pieces // 2, pieces // 2), :, pl.ds(0, feat)].reshape(feat, feat)
+    for n in range(feat // 128):
+        gb_o[:, pl.ds(n * 128, 128)] = grad_ref[0, pl.ds(n, 1), pl.ds(feat, 128)]
     hid_o[...] = hid_ref[...]
     fg_o[...] = fg_ref[...]
 
@@ -586,21 +601,21 @@
     scale = 1.0 / math.sqrt(owners * blocks * tile_rows)
 
     number = jnp.arange(tiles, dtype=jnp.int32)
-    hit = jnp.logical_and(
-        tile_dest[0][None, None, :] == jnp.arange(blocks, dtype=jnp.int32)[:, None, None],
-        tile_slot[0][None, None, :] == jnp.arange(owners, dtype=jnp.int32)[None, :, None],
+    code = tile_dest[0] * owners + tile_slot[0]
+    place = jnp.arange(blocks * owners, dtype=jnp.int32)
+    inverse = tiles + jnp.sum(
+        jnp.where(code[None, :] == place[:, None], number[None, :] - tiles, 0), axis=-1
     )
-    inverse = tiles + jnp.sum(jnp.where(hit, number - tiles, 0), axis=-1)
-    inverse = inverse.reshape(blocks * owners)
 
     vmem = pltpu.VMEM
     sem = pltpu.SemaphoreType.DMA
-    piece = (tall + 1, feat)
+    piece = (tall, feat + 128)
     scratch = [
-        vmem((blocks, 2, rows // 2, feat), BF16),
+        vmem((blocks, 4, 2, rows // 2, feat), BF16),
         vmem((blocks, rows, feat), BF16),
         vmem((tiles + 1, rows, tile_rows), BF16),
         vmem((owners, 2, rows // 2, feat), BF16),
+        vmem((nx * nc, 4, 2, rows // 2, feat), BF16),
         vmem((owners, 4, 2, rows // 2, feat), BF16),
         vmem((steps, total, chunk * tile_rows), BF16),
         vmem((total, feat), F32),
@@ -627,29 +642,31 @@
         vmem((nc, nx, nz, *piece), F32),
         sem((3,)),
         sem((3,)),
-        sem((owners,)),
-        sem((owners,)),
-        sem((steps, 2)),
-        sem((steps, 2)),
-        sem((steps, 2)),
-        sem((steps, 2)),
-        sem((steps, 2)),
-        sem((steps, 2)),
-        sem((steps, 2)),
-        sem((steps, 2)),
-        sem((owners,)),
-        sem((owners,)),
-        sem,
-        sem,
-        sem((nx,)),
-        sem((nx,)),
+        sem,
+        sem((steps,)),
+        sem,
+        sem,
+        sem,
+        sem((steps,)),
+        sem,
+        sem((steps,)),
+        sem,
+        sem((steps,)),
+        sem,
+        sem((steps,)),
+        sem,
+        sem((steps,)),
+        sem,
+        sem,
+        sem,
+        sem,
+        sem,
+        sem,
+        sem,
+        sem((4,)),
+        sem,
         sem((nz,)),
-        sem((nz,)),
-        sem((4,)),
-        sem((4,)),
-        sem((nz,)),
-        sem((nz,)),
-        sem((nx,)),
+        sem,
         sem((nx,)),
         sem,
         sem,
@@ -681,7 +698,7 @@
         cotangent,
     )
     hidden, grad_self, grad_neigh, grad_bias, feat_grad = pl.pallas_call(
-        functools.partial(finish_kernel, pieces, tall),
+        finish_kernel,
         out_shape=(
             jax.ShapeDtypeStruct((blocks, rows, feat), BF16),
             jax.ShapeDtypeStruct((feat, feat), F32),

time: 142 us -> 112 us (0.79)
  Pallas kernels: 139 us -> 109 us
    pallas_call x1, Pallas kernels: 136 us -> 106 us  [on_device(): pl.pallas_call(functools.partial(exchange_kernel, SPLIT, chunk, scale), o...]
where the time goes in v2:
time: 112 us; the launch traced here: 111 us
  Pallas kernels  109 us (97%)
  other arithmetic  1.6 us (1%)
    pallas_call x1, Pallas kernels, on_device(): pl.pallas_call(functools.partial(exchange_kernel, SPLIT, chunk, scale), o...  106 us
    pallas_call x1, Pallas kernels, on_device(): pl.pallas_call(finish_kernel, out_shape=(jax.ShapeDtypeStruct((blocks, ro...  2.25 us

profile of v2, /device:TPU:1, one launch (start us, length us, event | category | flops | bytes accessed | tf_op | source)
XLA Modules:
  0.0 110.8 jit_solution(16600939545867596955)
XLA Ops:
  0.6 0.7 multiply_add_fusion
  1.3 0.3 select_reduce_fusion
  1.6 0.6 broadcast_add_fusion.inv_ref
  2.2 106.3 %shard_map.128 = (bf16[16,32,256]{2,1,0:T(8,128)(2,1)}, bf16[16,32,256]{2,1,0:T(8,128)(2,1)}, f32[2,4,8,8,384]{4,3,2,1,0:T(8,128)}) custom-call(s32[64]{0:T(128)} %bitcast.12, s32[1024]{0:T(1024)} %broadcast_add_fusion.inv_ref, bf16[16,4,2,16,256]{4,3,2,1,0:T(8,128)(2,1)} %bitcast.8, bf16[512,32,128]{2,1,0:T(8,128)(2,1)} %bitcast.7, ...), custom_call_target="tpu_custom_call" | custom-call | tf_op jit(solution)/shard_map/pallas_call | solution.py:677
  108.5 2.3 %shard_map.129 = (bf16[16,32,256]{2,1,0:T(8,128)(2,1)}, f32[256,256]{1,0:T(8,128)}, f32[256,256]{1,0:T(8,128)}, f32[1,256]{1,0:T(1,128)}, bf16[16,32,256]{2,1,0:T(8,128)(2,1)}) custom-call(f32[64,8,384]{2,1,0:T(8,128)} %bitcast.9, bf16[16,32,256]{2,1,0:T(8,128)(2,1)} %get-tuple-element.14.hid_ref, bf16[16,32,256]{2,1,0:T(8,128)(2,1)} %get-tuple-element.15.fg_ref), custom_call_target="tpu_custom_call" | custom-call | tf_op jit(solution)/shard_map/pallas_call | solution.py:700
  (1 shorter events, 0.0 us)

commit v3 on v2

--- a/solution.py
+++ b/solution.py
@@ -10,10 +10,10 @@
 
 SPLIT = (4, 8, 2)
 CHUNK = 4
-LAG = 5
+LAG = 7
 HOP1, HOP2 = 2, 4
 
-GRADS_AT, GRADS_GAP = 3, 2
+GRADS_AT, GRADS_GAP = 1, 3
 
 MESH = pl.DeviceIdType.MESH
 F32 = jnp.float32

time: 112 us -> 109 us (0.973); the launches traced: 111 us -> 109 us
  Pallas kernels: 109 us -> 107 us
    pallas_call x1, Pallas kernels: 106 us -> 105 us  [on_device(): pl.pallas_call(functools.partial(exchange_kernel, SPLIT, chunk, scale), o...]
where the time goes in v3:
time: 109 us
  Pallas kernels  107 us (98%)
  other arithmetic  1.6 us (1%)
    pallas_call x1, Pallas kernels, on_device(): pl.pallas_call(functools.partial(exchange_kernel, SPLIT, chunk, scale), o...  105 us
    pallas_call x1, Pallas kernels, on_device(): pl.pallas_call(finish_kernel, out_shape=(jax.ShapeDtypeStruct((blocks, ro...  2.25 us

profile of v3, /device:TPU:1, one launch (start us, length us, event | category | flops | bytes accessed | tf_op | source)
XLA Modules:
  0.0 109.1 jit_solution(8695715972987841300)
XLA Ops:
  0.6 0.7 multiply_add_fusion
  1.3 0.3 select_reduce_fusion
  1.6 0.6 broadcast_add_fusion.inv_ref
  2.2 104.6 %shard_map.128 = (bf16[16,32,256]{2,1,0:T(8,128)(2,1)}, bf16[16,32,256]{2,1,0:T(8,128)(2,1)}, f32[2,4,8,8,384]{4,3,2,1,0:T(8,128)}) custom-call(s32[64]{0:T(128)} %bitcast.12, s32[1024]{0:T(1024)} %broadcast_add_fusion.inv_ref, bf16[16,4,2,16,256]{4,3,2,1,0:T(8,128)(2,1)} %bitcast.8, bf16[512,32,128]{2,1,0:T(8,128)(2,1)} %bitcast.7, ...), custom_call_target="tpu_custom_call" | custom-call | tf_op jit(solution)/shard_map/pallas_call | solution.py:677
  106.8 2.3 %shard_map.129 = (bf16[16,32,256]{2,1,0:T(8,128)(2,1)}, f32[256,256]{1,0:T(8,128)}, f32[256,256]{1,0:T(8,128)}, f32[1,256]{1,0:T(1,128)}, bf16[16,32,256]{2,1,0:T(8,128)(2,1)}) custom-call(f32[64,8,384]{2,1,0:T(8,128)} %bitcast.9, bf16[16,32,256]{2,1,0:T(8,128)(2,1)} %get-tuple-element.14.hid_ref, bf16[16,32,256]{2,1,0:T(8,128)(2,1)} %get-tuple-element.15.fg_ref), custom_call_target="tpu_custom_call" | custom-call | tf_op jit(solution)/shard_map/pallas_call | solution.py:700
  (1 shorter events, 0.0 us)
